TPU v7x, 32 devices: a whole 2x2x4 slice. The times are simulated.
32 devices in a mesh: slab: 2 (over x), pair: 8 (over z, y), quad: 2 (over core).
Axes of the slice: x: 2, y: 2, z: 4, core: 2. Of those that a mesh axis runs over, the one named last changes fastest.
Arguments:
- interferograms: float32 [64, 512, 1024], P(('pair', 'quad'), 'slab'), parts along dimension 1, may hold values from -24 to 24
- pair_epochs: int32 [2, 64], replicated, may hold values from 0 to 31, as said below
- days: int32 [32], replicated, may hold values from 0 to 732, as said below
Outputs:
- smoothed: float32 [32, 512, 1024], P(None, ('slab', 'pair'), 'quad'), parts along dimension 1
There are 2 independent parts, one for each index of `slab`. A program takes and returns all parts, laid end to end along the dimension named above; an argument that names none is the same for every part. Nothing has to cross between parts.
Inputs may be any that keep to these rules, and one draw needn't show every extreme that they name: pair_epochs[0, p] < pair_epochs[1, p] for every pair, the difference is at most 8, and every two consecutive epochs e, e + 1 form one of the pairs. days are strictly increasing, days[0] = 0, consecutive days differ by 12, 24 or 36, and the last day is always the maximum.
All inputs are finite; a program needn't handle non-finite values.
Results may differ from a plain program's by a relative error of at most 0.000071.
Values sent between devices are 32-bit elements; how exact they have to be, the bound alone decides.
No kernel may reach another device: no remote copies, remote signals or barrier semaphores. Data moves between devices by JAX's collectives and lax.ppermute only.
A program may use at most 64 MiB of HBM per device.

v0:
```python
import jax
import jax.numpy as jnp
from jax import lax
from jax.sharding import PartitionSpec as P

P_SIZE = 64
E = 32
RADIUS = 6


def padded_2(x, sides, width):
    for axis, dim in sides:
        devices, length = (lax.axis_size(axis), x.shape[dim])
        up = [(i, (i + 1) % devices) for i in range(devices - 1)]
        down = [(j, i) for i, j in up]
        last = lax.slice_in_dim(x, length - width, length, axis=dim)
        initial = lax.slice_in_dim(x, 0, width, axis=dim)
        before = lax.ppermute(last, axis, up)
        after = lax.ppermute(initial, axis, down)
        x = jnp.concatenate([before, x, after], axis=dim)
    return x


def pseudo_inverse(pair_epochs):
    first = pair_epochs[0]
    second = pair_epochs[1]
    steps_idx = jnp.arange(E - 1)
    design = (
        (first[:, None] <= steps_idx[None, :]) & (steps_idx[None, :] < second[:, None])
    ).astype(jnp.float32)
    normal = jnp.dot(design.T, design, precision=lax.Precision.HIGHEST)
    factor = jnp.linalg.cholesky(normal)
    return jax.scipy.linalg.cho_solve((factor, True), design.T)


def trend_basis(days):
    times = days.astype(jnp.float32)
    scaled = (times - jnp.mean(times)) / 365.25
    phase = 2.0 * jnp.pi * times / 365.25
    basis = jnp.stack([jnp.ones_like(times), scaled, jnp.sin(phase), jnp.cos(phase)], axis=1)
    factor = jnp.linalg.cholesky(jnp.dot(basis.T, basis, precision=lax.Precision.HIGHEST))
    return (basis, factor)


def gauss_taps():
    offsets = (jnp.arange(2 * RADIUS + 1) - RADIUS).astype(jnp.float32)
    weights = jnp.exp(-offsets * offsets / 8.0)
    return weights / jnp.sum(weights)


def taps_columns(padded, count):
    taps = gauss_taps()
    total = taps[0] * padded[:, :, 0:count]
    for shift in range(1, 2 * RADIUS + 1):
        total = total + taps[shift] * padded[:, :, shift : shift + count]
    return total


def taps_rows(padded, count):
    taps = gauss_taps()
    total = taps[0] * padded[:, 0:count, :]
    for shift in range(1, 2 * RADIUS + 1):
        total = total + taps[shift] * padded[:, shift : shift + count, :]
    return total


def shards(interferograms, pair_epochs, days):
    n_pair = lax.axis_size("pair")
    n_quad = lax.axis_size("quad")
    local = interferograms.shape[0]
    height = interferograms.shape[1]
    width = interferograms.shape[2]
    rows = height // n_pair
    cols = width // n_quad
    blocks = interferograms.reshape(local, n_pair, rows, n_quad, cols)
    blocks = blocks.transpose(1, 3, 0, 2, 4).reshape(n_pair * n_quad * local, rows, cols)
    stacks = lax.all_to_all(blocks, ("pair", "quad"), split_axis=0, concat_axis=0, tiled=True)
    flat = stacks.reshape(P_SIZE, rows * cols)
    pinv = pseudo_inverse(pair_epochs)
    basis, factor = trend_basis(days)
    increments = jnp.dot(pinv, flat, precision=lax.Precision.HIGHEST)
    displacement = jnp.concatenate(
        [jnp.zeros((1, rows * cols), jnp.float32), jnp.cumsum(increments, axis=0)], axis=0
    )
    coefficients = jax.scipy.linalg.cho_solve(
        (factor, True), jnp.dot(basis.T, displacement, precision=lax.Precision.HIGHEST)
    )
    detrended = displacement - jnp.dot(basis, coefficients, precision=lax.Precision.HIGHEST)
    detrended = detrended.reshape(E, rows, cols)
    widened = padded_2(detrended, (("quad", 2),), RADIUS)
    across = taps_columns(widened, cols)
    heightened = padded_2(across, (("pair", 1),), RADIUS)
    smoothed = taps_rows(heightened, rows)
    return smoothed


def solution(mesh):
    placed = (P(("pair", "quad"), "slab", None), P(), P())
    return jax.shard_map(
        shards,
        mesh=mesh,
        in_specs=placed,
        out_specs=P(None, ("slab", "pair"), "quad"),
        check_vma=False,
    )
```

profile of v0, /device:TPU:19, one launch (start us, length us, event | category | flops | bytes accessed | tf_op | source)
XLA Modules:
  0.0 191.6 jit_solution(10135328722315464915)
XLA Ops:
  0.0 6.6 %reshape.39 = f32[4,8,32,2,512]{4,3,2,1,0:T(2,128)} reshape(f32[4,256,1024]{2,1,0:T(8,128)} %param.3) | data formatting | bytes 8388608 | tf_op jit(solution)/shard_map/reshape | solution.py:75
  6.6 4.9 %copy.11 = f32[8,2,4,32,512]{4,3,2,1,0:T(8,128)} copy(f32[8,2,4,32,512]{4,1,3,0,2:T(2,128)} %bitcast.65) | data formatting | bytes 8388608 | tf_op jit(solution)/shard_map/transpose | solution.py:76
  11.5 6.6 %all-to-all-start = ((f32[64,32,512]{2,1,0:T(8,128)}), f32[64,32,512]{2,1,0:T(8,128)}, u32[]{:S(2)}, u32[]{:S(2)}) async-start(f32[64,32,512]{2,1,0:T(8,128)} %bitcast.63), calls=%async_computation | async-start | bytes 8388608 | tf_op jit(solution)/shard_map/all_to_all | solution.py:77
  18.5 2.8 %cholesky.29 = f32[31,31]{1,0:T(8,128)S(1)} custom-call(f32[31,31]{1,0:T(8,128)S(1)} %fusion.68), custom_call_target="Cholesky" | custom-call | tf_op jit(solution)/shard_map/jit(cholesky)/cholesky | solution.py:32
  22.6 2.4 %custom-call.20 = f32[1,31,31]{1,2,0:T(8,128)S(1)} custom-call(f32[1,31,31]{2,1,0:T(8,128)S(1)} %fusion.64), custom_call_target="InvertDiagBlocksLowerTriangular" | custom-call | tf_op jit(solution)/shard_map/jit(_cho_solve)/triangular_solve | solution.py:33
  28.7 0.7 fusion.81
  30.1 0.7 fusion.86
  31.2 79.0 %all-to-all-done = f32[64,32,512]{2,1,0:T(8,128)} async-done(((f32[64,32,512]{2,1,0:T(8,128)}), f32[64,32,512]{2,1,0:T(8,128)}, u32[]{:S(2)}, u32[]{:S(2)}) %all-to-all-start) | async-done | bytes 4194336 | tf_op jit(solution)/shard_map/all_to_all | solution.py:77
  110.2 4.6 %copy.14 = f32[8,8,32,512]{3,1,2,0:T(8,128)S(1)} copy(f32[8,8,32,512]{3,2,1,0:T(8,128)} %bitcast.29) | data formatting | bytes 8388608
  114.8 3.4 %fusion.87 = f32[31,16384]{1,0:T(8,128)} fusion(f32[31,64]{1,0:T(8,128)S(1)} %fusion.65, f32[64,16384]{1,0:T(8,128)S(1)} %bitcast.64), kind=kOutput, calls=%fused_computation.151 | convolution fusion | flops 390070272 | bytes 6233856 | tf_op jit(solution)/shard_map/dot_general | solution.py:81
  118.2 3.4 %reduce_window_sum.11 = f32[31,16384]{1,0:T(8,128)S(1)} reduce-window(f32[31,16384]{1,0:T(8,128)} %fusion.87, f32[]{:T(128)} %constant.108.clone.1), window={size=31x1 pad=30_0x0_0}, to_apply=%region_3.4 | reduce-window | flops 15237120 | bytes 4063236 | tf_op jit(solution)/shard_map/jit(cumsum)/reduce_window_sum | solution.py:83
  121.6 1.2 fusion.57
  122.8 0.7 fusion.74
  124.1 2.1 %convolution_subtract_fusion = f32[32,16384]{1,0:T(8,128)S(1)} fusion(f32[4,16384]{1,0:T(4,128)S(1)} %fusion.76, f32[31,16384]{1,0:T(8,128)S(1)} %reduce_window_sum.11, f32[32,1]{0,1:T(1,128)S(1)} %get-tuple-element.25, f32[32,1]{0,1:T(1,128)S(1)} %get-tuple-element.26, f32[32,1]{0,1:T(1,128)S(1)} %get-tuple-element.24, f32[4]{0:T(128)S(1)} %pad.7.clone), kind=kOutput, calls=%fused_computation | convolution fusion | flops 25690496 | bytes 4391312 | tf_op jit(solution)/shard_map/dot_general | solution.py:88
  126.2 1.4 copy.15
  127.9 2.9 %collective-permute-start.1 = (f32[32,32,6]{2,1,0:T(8,128)S(1)}, f32[32,32,6]{2,1,0:T(8,128)S(1)}, u32[]{:S(2)}, u32[]{:S(2)}) collective-permute-start(f32[32,32,6]{2,1,0:T(8,128)S(1)} %get-tuple-element.7), channel_id=1, source_target_pairs={{1,0},{3,2},{5,4},{7,6},{9,8},{11,10},{13,12},{15,14},{17,16},{19,... | collective-permute-start | bytes 73736 | tf_op jit(solution)/shard_map/ppermute | solution.py:19
  131.0 1.3 collective-permute-start
  132.3 2.4 %collective-permute-done = f32[32,32,6]{2,1,0:T(8,128)S(1)} collective-permute-done((f32[32,32,6]{2,1,0:T(8,128)S(1)}, f32[32,32,6]{2,1,0:T(8,128)S(1)}, u32[]{:S(2)}, u32[]{:S(2)}) %collective-permute-start) | collective-permute-done | bytes 24608 | tf_op jit(solution)/shard_map/ppermute | solution.py:18
  134.8 15.6 %fusion.42 = f32[32,32,512]{2,1,0:T(8,128)S(1)} fusion(f32[32,32,512]{2,1,0:T(8,128)S(1)} %bitcast.62, f32[32,32,6]{2,1,0:T(8,128)S(1)} %collective-permute-done, f32[32,32,518]{2,1,0:T(8,128)S(1)} %constant_dynamic-update-slice_fusion, f32[]{:T(128)} %bitcast.25, f32[]{:T(128)} %bitcast.24, f32[]{:T(128)} %bitcast.23, f32[]{:T(128)} %bitcast.22, ...), kind=kLoop, calls=%fused_computation.73 | loop fusion | flops 16252928 | bytes 16801844 | tf_op jit(solution)/shard_map/add | solution.py:55
  150.6 1.9 %collective-permute-start.2 = (f32[32,6,512]{2,1,0:T(8,128)S(1)}, f32[32,6,512]{2,1,0:T(8,128)S(1)}, u32[]{:S(2)}, u32[]{:S(2)}) collective-permute-start(f32[32,6,512]{2,1,0:T(8,128)S(1)} %get-tuple-element.5), channel_id=1, source_target_pairs={{0,2},{2,4},{4,6},{6,8},{8,10},{10,12},{12,14},{1,3},{3,5},{5,7},{... | collective-permute-start | bytes 1179656 | tf_op jit(solution)/shard_map/ppermute | solution.py:18
  152.5 4.3 %collective-permute-start.3 = (f32[32,6,512]{2,1,0:T(8,128)S(1)}, f32[32,6,512]{2,1,0:T(8,128)S(1)}, u32[]{:S(2)}, u32[]{:S(2)}) collective-permute-start(f32[32,6,512]{2,1,0:T(8,128)S(1)} %get-tuple-element.6), channel_id=1, source_target_pairs={{2,0},{4,2},{6,4},{8,6},{10,8},{12,10},{14,12},{3,1},{5,3},{7,5},{... | collective-permute-start | bytes 1179656 | tf_op jit(solution)/shard_map/ppermute | solution.py:19
  156.8 18.4 %collective-permute-done.2 = f32[32,6,512]{2,1,0:T(8,128)S(1)} collective-permute-done((f32[32,6,512]{2,1,0:T(8,128)S(1)}, f32[32,6,512]{2,1,0:T(8,128)S(1)}, u32[]{:S(2)}, u32[]{:S(2)}) %collective-permute-start.2) | collective-permute-done | bytes 393248 | tf_op jit(solution)/shard_map/ppermute | solution.py:18
  175.1 3.4 %collective-permute-done.3 = f32[32,6,512]{2,1,0:T(8,128)S(1)} collective-permute-done((f32[32,6,512]{2,1,0:T(8,128)S(1)}, f32[32,6,512]{2,1,0:T(8,128)S(1)}, u32[]{:S(2)}, u32[]{:S(2)}) %collective-permute-start.3) | collective-permute-done | bytes 393248 | tf_op jit(solution)/shard_map/ppermute | solution.py:19
  178.5 13.1 %fusion.3 = f32[32,32,512]{2,1,0:T(8,128)} fusion(f32[32,32,512]{2,1,0:T(8,128)S(1)} %fusion.42, f32[32,6,512]{2,1,0:T(8,128)S(1)} %collective-permute-done.3, f32[32,6,512]{2,1,0:T(8,128)S(1)} %collective-permute-done.2, f32[]{:T(128)} %bitcast.25, f32[]{:T(128)} %bitcast.24, f32[]{:T(128)} %bitcast.23, f32[]{:T(128)} %bitcast.22, f32[]{:T(128)} %bitcast.21, ...), kind=kLoop, calls=%fused_computation.34 | loop fusion | flops 19398656 | bytes 4980788 | tf_op jit(solution)/shard_map/add | solution.py:63
  (31 shorter events, 6.9 us)
Async XLA Ops:
  11.5 6.6 %copy-start = (s32[2,64]{1,0:T(2,128)S(1)}, s32[2,64]{1,0:T(2,128)}, u32[]{:S(2)}) copy-start(s32[2,64]{1,0:T(2,128)} %param.4) | copy-start | bytes 1540
  11.5 13.5 %copy-start.1 = (s32[32]{0:T(128)S(1)}, s32[32]{0:T(128)}, u32[]{:S(2)}) copy-start(s32[32]{0:T(128)} %param.5) | copy-start | bytes 388
  11.5 98.7 %all-to-all-start = ((f32[64,32,512]{2,1,0:T(8,128)}), f32[64,32,512]{2,1,0:T(8,128)}, u32[]{:S(2)}, u32[]{:S(2)}) async-start(f32[64,32,512]{2,1,0:T(8,128)} %bitcast.63), calls=%async_computation | async-start | bytes 8388608 | tf_op jit(solution)/shard_map/all_to_all | solution.py:77
  127.9 4.4 %collective-permute-start.1 = (f32[32,32,6]{2,1,0:T(8,128)S(1)}, f32[32,32,6]{2,1,0:T(8,128)S(1)}, u32[]{:S(2)}, u32[]{:S(2)}) collective-permute-start(f32[32,32,6]{2,1,0:T(8,128)S(1)} %get-tuple-element.7), channel_id=1, source_target_pairs={{1,0},{3,2},{5,4},{7,6},{9,8},{11,10},{13,12},{15,14},{17,16},{19,... | collective-permute-start | bytes 73736 | tf_op jit(solution)/shard_map/ppermute | solution.py:19
  131.0 3.8 %collective-permute-start = (f32[32,32,6]{2,1,0:T(8,128)S(1)}, f32[32,32,6]{2,1,0:T(8,128)S(1)}, u32[]{:S(2)}, u32[]{:S(2)}) collective-permute-start(f32[32,32,6]{2,1,0:T(8,128)S(1)} %get-tuple-element.8), channel_id=1, source_target_pairs={{0,1},{2,3},{4,5},{6,7},{8,9},{10,11},{12,13},{14,15},{16,17},{18,... | collective-permute-start | bytes 73736 | tf_op jit(solution)/shard_map/ppermute | solution.py:18
  150.6 24.6 %collective-permute-start.2 = (f32[32,6,512]{2,1,0:T(8,128)S(1)}, f32[32,6,512]{2,1,0:T(8,128)S(1)}, u32[]{:S(2)}, u32[]{:S(2)}) collective-permute-start(f32[32,6,512]{2,1,0:T(8,128)S(1)} %get-tuple-element.5), channel_id=1, source_target_pairs={{0,2},{2,4},{4,6},{6,8},{8,10},{10,12},{12,14},{1,3},{3,5},{5,7},{... | collective-permute-start | bytes 1179656 | tf_op jit(solution)/shard_map/ppermute | solution.py:18
  152.5 26.0 %collective-permute-start.3 = (f32[32,6,512]{2,1,0:T(8,128)S(1)}, f32[32,6,512]{2,1,0:T(8,128)S(1)}, u32[]{:S(2)}, u32[]{:S(2)}) collective-permute-start(f32[32,6,512]{2,1,0:T(8,128)S(1)} %get-tuple-element.6), channel_id=1, source_target_pairs={{2,0},{4,2},{6,4},{8,6},{10,8},{12,10},{14,12},{3,1},{5,3},{7,5},{... | collective-permute-start | bytes 1179656 | tf_op jit(solution)/shard_map/ppermute | solution.py:19
where the time goes:
time: 192 us
  waiting for transfers between devices  103 us (54%)
  other arithmetic  42.8 us (22%)
  local copies, waits for them, and re-layouts  19 us (10%)
  starting transfers between devices  17 us (9%)
  matrix products  8.82 us (5%)
    all_to_all x1, waiting for transfers between devices, shards(): lax.all_to_all(blocks, ('pair', 'quad'), split_axis=0, concat_axis=0, til...  79 us
    ppermute x2, waiting for transfers between devices, padded_2(): before = lax.ppermute(last, axis, up)  20.8 us
    add x1, other arithmetic, taps_columns(): total = total + taps[shift] * padded[:, :, shift:shift + count]  15.6 us
    add x1, other arithmetic, taps_rows(): total = total + taps[shift] * padded[:, shift:shift + count, :]  13.1 us
    ppermute x2, starting transfers between devices, padded_2(): after = lax.ppermute(initial, axis, down)  7.17 us
    all_to_all x1, starting transfers between devices, shards(): lax.all_to_all(blocks, ('pair', 'quad'), split_axis=0, concat_axis=0, til...  6.6 us
    reshape x1, local copies, waits for them, and re-layouts, shards(): blocks = interferograms.reshape(local, n_pair, rows, n_quad, cols)  6.57 us
    unnamed x7, local copies, waits for them, and re-layouts  6.27 us
  transfers between devices with their start and end apart: 5, of which 4 were waited for; matrix products, arithmetic and copies ran while one was open for 7% of the time, Pallas kernels for 0%

commit v1 on v0

v1 whole, which is shorter than its diff:
```python
import functools

import jax
import jax.numpy as jnp
from jax import lax
from jax.experimental import pallas as pl
from jax.experimental.pallas import tpu as pltpu
from jax.sharding import PartitionSpec as P

E = 32
RADIUS = 6
SUB = 8
LANE = 128
HIGHEST = lax.Precision.HIGHEST


def pseudo_inverse(pair_epochs):
    first = pair_epochs[0]
    second = pair_epochs[1]
    steps_idx = jnp.arange(E - 1)
    design = (
        (first[:, None] <= steps_idx[None, :]) & (steps_idx[None, :] < second[:, None])
    ).astype(jnp.float32)
    normal = jnp.dot(design.T, design, precision=HIGHEST)
    factor = jnp.linalg.cholesky(normal)
    return jax.scipy.linalg.cho_solve((factor, True), design.T)


def trend_basis(days):
    times = days.astype(jnp.float32)
    scaled = (times - jnp.mean(times)) / 365.25
    phase = 2.0 * jnp.pi * times / 365.25
    basis = jnp.stack([jnp.ones_like(times), scaled, jnp.sin(phase), jnp.cos(phase)], axis=1)
    factor = jnp.linalg.cholesky(jnp.dot(basis.T, basis, precision=HIGHEST))
    return (basis, factor)


def temporal_operator(pair_epochs, days):
    pinv = pseudo_inverse(pair_epochs)
    steps = jnp.concatenate(
        [jnp.zeros((1, pinv.shape[1]), jnp.float32), jnp.cumsum(pinv, axis=0)], axis=0
    )
    basis, factor = trend_basis(days)
    coefficients = jax.scipy.linalg.cho_solve(
        (factor, True), jnp.dot(basis.T, steps, precision=HIGHEST)
    )
    return steps - jnp.dot(basis, coefficients, precision=HIGHEST)


def window(start, length, extent, align):
    low = max(0, (start - RADIUS) // align * align)
    high = min(extent, -(-(start + length + RADIUS) // align) * align)
    return low, high


def tap_sum():
    return sum(jnp.exp(jnp.float32(-(i * i) / 8.0)) for i in range(-RADIUS, RADIUS + 1))


def band(shape, along, offset):
    one = lax.broadcasted_iota(jnp.int32, shape, along) + offset
    other = lax.broadcasted_iota(jnp.int32, shape, 1 - along)
    apart = one - other
    far = apart.astype(jnp.float32)
    weights = jnp.exp(far * far * -0.125) / tap_sum()
    return jnp.where(jnp.abs(apart) <= RADIUS, weights, 0.0)


def smooth_body(rows, cols, x_ref, out_ref, mid_ref):
    height, width = x_ref.shape[1:]
    n_quad = width // cols
    tall = min(256, height)
    wide = min(256, cols)
    bands = {}

    def banded(shape, along, offset):
        key = (shape, along, offset)
        if key not in bands:
            bands[key] = band(shape, along, offset)
        return bands[key]

    for r0 in range(0, height, tall):
        low, high = window(r0, tall, height, SUB)
        weights = banded((tall, high - low), 0, r0 - low)
        mid_ref[r0 : r0 + tall, :] = jnp.dot(
            weights, x_ref[0, low:high, :], precision=HIGHEST, preferred_element_type=jnp.float32
        )
    for c0 in range(0, width, wide):
        low, high = window(c0, wide, width, LANE)
        weights = banded((high - low, wide), 1, c0 - low)
        done = jnp.dot(
            mid_ref[:, low:high], weights, precision=HIGHEST, preferred_element_type=jnp.float32
        )
        quad, at = c0 // cols, c0 % cols
        for block in range(height // rows):
            out_ref[block * n_quad + quad, :, at : at + wide] = done[
                block * rows : (block + 1) * rows, :
            ]


def smooth_pair(interferograms, index, rows, cols):
    height, width = interferograms.shape[1:]
    blocks = (height // rows) * (width // cols)
    return pl.pallas_call(
        functools.partial(smooth_body, rows, cols),
        grid=(1,),
        in_specs=[pl.BlockSpec((1, height, width), lambda i: (index, 0, 0))],
        out_specs=pl.BlockSpec((blocks, rows, cols), lambda i: (0, 0, 0)),
        out_shape=jax.ShapeDtypeStruct((blocks, rows, cols), jnp.float32),
        scratch_shapes=[pltpu.VMEM((height, width), jnp.float32)],
        cost_estimate=pl.CostEstimate(
            flops=2 * height * width * 6 * 768,
            bytes_accessed=8 * height * width,
            transcendentals=0,
        ),
        name="smooth",
    )(interferograms)


def apply_body(n_in, has_acc, *refs):
    w_refs, x_refs = refs[:n_in], refs[n_in : 2 * n_in]
    out_ref = refs[-1]
    cols = out_ref.shape[-1]
    total = None
    for w_ref, x_ref in zip(w_refs, x_refs):
        x = x_ref[...].reshape(-1, cols)
        part = jnp.dot(w_ref[...], x, precision=HIGHEST, preferred_element_type=jnp.float32)
        total = part if total is None else total + part
    total = total.reshape(out_ref.shape)
    if has_acc:
        total = total + refs[2 * n_in][...]
    out_ref[...] = total


def apply_operator(weights, stacks, acc):
    pairs, rows, cols = stacks[0].shape
    epochs = weights[0].shape[0] // SUB
    n_in = len(stacks)
    moving = pl.BlockSpec((pairs, SUB, cols), lambda i: (0, i, 0))
    fixed = pl.BlockSpec((epochs * SUB, pairs * SUB), lambda i: (0, 0))
    out_spec = pl.BlockSpec((epochs, SUB, cols), lambda i: (0, i, 0))
    extra = [] if acc is None else [acc]
    return pl.pallas_call(
        functools.partial(apply_body, n_in, acc is not None),
        grid=(rows // SUB,),
        in_specs=[fixed] * n_in + [moving] * n_in + [out_spec] * len(extra),
        out_specs=out_spec,
        out_shape=jax.ShapeDtypeStruct((epochs, rows, cols), jnp.float32),
        cost_estimate=pl.CostEstimate(
            flops=2 * 6 * SUB * epochs * pairs * rows * cols * n_in,
            bytes_accessed=4 * rows * cols * (pairs * n_in + epochs),
            transcendentals=0,
        ),
        name="apply",
    )(*weights, *stacks, *extra)


def shards(interferograms, pair_epochs, days):
    n_pair = lax.axis_size("pair")
    n_quad = lax.axis_size("quad")
    local, height, width = interferograms.shape
    rows = height // n_pair
    cols = width // n_quad
    stacks = []
    for index in range(local):
        blocks = smooth_pair(interferograms, index, rows, cols)
        stacks.append(
            lax.all_to_all(blocks, ("pair", "quad"), split_axis=0, concat_axis=0, tiled=True)
        )
    operator = temporal_operator(pair_epochs, days)
    eye = jnp.eye(SUB, dtype=jnp.float32)
    weights = []
    for index in range(local):
        part = operator[:, index::local]
        spread = part[:, None, :, None] * eye[None, :, None, :]
        weights.append(spread.reshape(E * SUB, -1))
    total = None
    if local > 1:
        total = apply_operator(weights[:-1], stacks[:-1], None)
    return apply_operator(weights[-1:], stacks[-1:], total)


def solution(mesh):
    placed = (P(("pair", "quad"), "slab", None), P(), P())
    return jax.shard_map(
        shards,
        mesh=mesh,
        in_specs=placed,
        out_specs=P(None, ("slab", "pair"), "quad"),
        check_vma=False,
    )
```

time: 192 us -> 133 us (0.69)
  waiting for transfers between devices: 103 us -> 48.7 us
  Pallas kernels: 0 us -> 32.6 us
  other arithmetic: 42.8 us -> 12.9 us
  matrix products: 8.82 us -> 1.65 us
  local copies, waits for them, and re-layouts: 19 us -> 13 us
  starting transfers between devices: 17 us -> 21.8 us
    pallas_call x0 -> x6, Pallas kernels: none -> 32.6 us  [the longest x4 19.8 us: smooth_pair(): pl.pallas_call(functools.partial(smooth_body, rows, cols), grid=(1,), in_...]
    all_to_all x1 -> x4, waiting for transfers between devices: 79 us -> 48.7 us  [shards(): lax.all_to_all(blocks, ('pair', 'quad'), split_axis=0, concat_axis=0, til...]
    add x2 -> x0, other arithmetic: 28.8 us -> none  [the longest x1 15.6 us: taps_columns(): total = total + taps[shift] * padded[:, :, shift:shift + count]]
    ppermute x4 -> x0, waiting for transfers between devices: 24.2 us -> none  [the longest x2 20.8 us: padded_2(): before = lax.ppermute(last, axis, up)]
    all_to_all x1 -> x4, starting transfers between devices: 6.6 us -> 21.8 us  [shards(): lax.all_to_all(blocks, ('pair', 'quad'), split_axis=0, concat_axis=0, til...]
    mul x0 -> x4, local copies, waits for them, and re-layouts: none -> 11.3 us  [shards(): spread = part[:, None, :, None] * eye[None, :, None, :]]
    ppermute x4 -> x0, starting transfers between devices: 10.4 us -> none  [the longest x2 7.17 us: padded_2(): after = lax.ppermute(initial, axis, down)]
    reshape x1 -> x0, local copies, waits for them, and re-layouts: 6.57 us -> none  [shards(): blocks = interferograms.reshape(local, n_pair, rows, n_quad, cols)]
  transfers between devices with their start and end apart: 5 -> 4, of which waited for: 4 -> 3; matrix products, arithmetic and copies ran while one was open for 7% -> 20% of each run, Pallas kernels for 0% -> 17%
where the time goes in v1:
time: 133 us; the launch traced here: 132 us
  waiting for transfers between devices  48.7 us (37%)
  Pallas kernels  32.6 us (25%)
  starting transfers between devices  21.8 us (16%)
  local copies, waits for them, and re-layouts  13 us (10%)
  other arithmetic  12.9 us (10%)
  matrix products  1.65 us (1%)
    all_to_all x4, waiting for transfers between devices, shards(): lax.all_to_all(blocks, ('pair', 'quad'), split_axis=0, concat_axis=0, til...  48.7 us
    all_to_all x4, starting transfers between devices, shards(): lax.all_to_all(blocks, ('pair', 'quad'), split_axis=0, concat_axis=0, til...  21.8 us
    pallas_call x4, Pallas kernels, smooth_pair(): pl.pallas_call(functools.partial(smooth_body, rows, cols), grid=(1,), in_...  19.8 us
    pallas_call x2, Pallas kernels, apply_operator(): pl.pallas_call(functools.partial(apply_body, n_in, acc is not None), grid...  12.8 us
    mul x4, local copies, waits for them, and re-layouts, shards(): spread = part[:, None, :, None] * eye[None, :, None, :]  11.3 us
    another operation x3, other arithmetic, pseudo_inverse(): factor = jnp.linalg.cholesky(normal)  3.58 us
    mul x1, other arithmetic, shards(): spread = part[:, None, :, None] * eye[None, :, None, :]  3.29 us
    another operation x2, other arithmetic, pseudo_inverse(): return jax.scipy.linalg.cho_solve((factor, True), design.T)  3.05 us
  transfers between devices with their start and end apart: 4, of which 3 were waited for; matrix products, arithmetic and copies ran while one was open for 20% of the time, Pallas kernels for 17%

profile of v1, /device:TPU:19, one launch (start us, length us, event | category | flops | bytes accessed | tf_op | source)
XLA Modules:
  0.0 131.5 jit_solution(3391549556494658737)
XLA Ops:
  0.0 4.9 %smooth.5 = f32[16,32,512]{2,1,0:T(8,128)} custom-call(f32[4,256,1024]{2,1,0:T(8,128)} %x_ref.7), custom_call_target="tpu_custom_call" | custom-call | flops 2415919104 | bytes 2097152 | tf_op jit(solution)/shard_map/smooth/pallas_call | solution.py:104
  4.9 6.5 %all-to-all-start.1 = ((f32[16,32,512]{2,1,0:T(8,128)}), f32[16,32,512]{2,1,0:T(8,128)S(1)}, u32[]{:S(2)}, u32[]{:S(2)}) async-start(f32[16,32,512]{2,1,0:T(8,128)} %smooth.5), calls=%async_computation.1 | async-start | bytes 2097152 | tf_op jit(solution)/shard_map/all_to_all | solution.py:168
  11.4 4.9 %smooth.6 = f32[16,32,512]{2,1,0:T(8,128)} custom-call(f32[4,256,1024]{2,1,0:T(8,128)} %x_ref.7), custom_call_target="tpu_custom_call" | custom-call | flops 2415919104 | bytes 2097152 | tf_op jit(solution)/shard_map/smooth/pallas_call | solution.py:104
  16.3 19.6 %all-to-all-done.1.refs_3_ = f32[16,32,512]{2,1,0:T(8,128)S(1)} async-done(((f32[16,32,512]{2,1,0:T(8,128)}), f32[16,32,512]{2,1,0:T(8,128)S(1)}, u32[]{:S(2)}, u32[]{:S(2)}) %all-to-all-start.1) | async-done | bytes 1048608 | tf_op jit(solution)/shard_map/all_to_all | solution.py:168
  36.0 5.1 %all-to-all-start.2 = ((f32[16,32,512]{2,1,0:T(8,128)}), f32[16,32,512]{2,1,0:T(8,128)S(1)}, u32[]{:S(2)}, u32[]{:S(2)}) async-start(f32[16,32,512]{2,1,0:T(8,128)} %smooth.6), calls=%async_computation.2 | async-start | bytes 2097152 | tf_op jit(solution)/shard_map/all_to_all | solution.py:168
  41.5 4.9 %smooth.7 = f32[16,32,512]{2,1,0:T(8,128)} custom-call(f32[4,256,1024]{2,1,0:T(8,128)} %x_ref.7), custom_call_target="tpu_custom_call" | custom-call | flops 2415919104 | bytes 2097152 | tf_op jit(solution)/shard_map/smooth/pallas_call | solution.py:104
  46.4 19.3 %all-to-all-done.2.refs_4_ = f32[16,32,512]{2,1,0:T(8,128)S(1)} async-done(((f32[16,32,512]{2,1,0:T(8,128)}), f32[16,32,512]{2,1,0:T(8,128)S(1)}, u32[]{:S(2)}, u32[]{:S(2)}) %all-to-all-start.2) | async-done | bytes 1048608 | tf_op jit(solution)/shard_map/all_to_all | solution.py:168
  65.6 5.1 %all-to-all-start.3 = ((f32[16,32,512]{2,1,0:T(8,128)}), f32[16,32,512]{2,1,0:T(8,128)S(1)}, u32[]{:S(2)}, u32[]{:S(2)}) async-start(f32[16,32,512]{2,1,0:T(8,128)} %smooth.7), calls=%async_computation.3 | async-start | bytes 2097152 | tf_op jit(solution)/shard_map/all_to_all | solution.py:168
  70.8 2.8 %cholesky.29 = f32[31,31]{1,0:T(8,128)S(1)} custom-call(f32[31,31]{1,0:T(8,128)S(1)} %fusion.9), custom_call_target="Cholesky" | custom-call | tf_op jit(solution)/shard_map/jit(cholesky)/cholesky | solution.py:25
  73.6 0.7 compare_reduce_fusion.1
  75.1 2.4 %custom-call.20 = f32[1,31,31]{1,2,0:T(8,128)S(1)} custom-call(f32[1,31,31]{2,1,0:T(8,128)S(1)} %fusion.5), custom_call_target="InvertDiagBlocksLowerTriangular" | custom-call | tf_op jit(solution)/shard_map/jit(_cho_solve)/triangular_solve | solution.py:26
  77.4 0.7 convert_reduce_fusion
  79.6 0.7 compare_reduce_fusion
  80.5 5.0 %smooth.4 = f32[16,32,512]{2,1,0:T(8,128)} custom-call(f32[4,256,1024]{2,1,0:T(8,128)} %x_ref.7), custom_call_target="tpu_custom_call" | custom-call | flops 2415919104 | bytes 2097152 | tf_op jit(solution)/shard_map/smooth/pallas_call | solution.py:104
  85.5 9.8 %all-to-all-done.3.refs_5_ = f32[16,32,512]{2,1,0:T(8,128)S(1)} async-done(((f32[16,32,512]{2,1,0:T(8,128)}), f32[16,32,512]{2,1,0:T(8,128)S(1)}, u32[]{:S(2)}, u32[]{:S(2)}) %all-to-all-start.3) | async-done | bytes 1048608 | tf_op jit(solution)/shard_map/all_to_all | solution.py:168
  95.3 5.1 %all-to-all-start = ((f32[16,32,512]{2,1,0:T(8,128)}), f32[16,32,512]{2,1,0:T(8,128)S(1)}, u32[]{:S(2)}, u32[]{:S(2)}) async-start(f32[16,32,512]{2,1,0:T(8,128)} %smooth.4), calls=%async_computation | async-start | bytes 2097152 | tf_op jit(solution)/shard_map/all_to_all | solution.py:168
  103.1 3.3 %broadcast_multiply_fusion = (f32[32,8,16,8]{3,2,1,0:T(8,128)}, f32[32,8,16,8]{3,2,1,0:T(8,128)}, f32[32,8,16,8]{3,2,1,0:T(8,128)}, f32[32,8,16,8]{3,2,1,0:T(8,128)S(1)}) fusion(f32[32,16]{1,0:T(8,128)S(1)} %slice.59, f32[8,8]{1,0:T(8,128)S(1)} %fusion.16, f32[32,16]{1,0:T(8,128)S(1)} %slice.57, f32[32,16]{1,0:T(8,128)S(1)} %slice.58, f32[32,16]{1,0:T(8,128)S(1)} %slice.56), kind=kLoop, calls=%fused_computation.1 | loop fusion | flops 131072 | bytes 532736 | tf_op jit(solution)/shard_map/mul | solution.py:175
  106.4 3.2 %mul.76.refs_0_ = f32[256,128]{1,0:T(8,128)} reshape(f32[32,8,16,8]{3,2,1,0:T(8,128)} %get-tuple-element.6) | data formatting | bytes 262144 | tf_op jit(solution)/shard_map/mul | solution.py:175
  109.7 3.2 %mul.79.refs_1_ = f32[256,128]{1,0:T(8,128)} reshape(f32[32,8,16,8]{3,2,1,0:T(8,128)} %get-tuple-element.7) | data formatting | bytes 262144 | tf_op jit(solution)/shard_map/mul | solution.py:175
  112.9 3.2 %mul.82.refs_2_ = f32[256,128]{1,0:T(8,128)} reshape(f32[32,8,16,8]{3,2,1,0:T(8,128)} %get-tuple-element.5) | data formatting | bytes 262144 | tf_op jit(solution)/shard_map/mul | solution.py:175
  116.1 1.6 %mul.73.refs_0_ = f32[256,128]{1,0:T(8,128)} reshape(f32[32,8,16,8]{3,2,1,0:T(8,128)S(1)} %get-tuple-element.8) | data formatting | bytes 262144 | tf_op jit(solution)/shard_map/mul | solution.py:175
  117.7 7.8 %apply.2.refs_2_ = f32[32,32,512]{2,1,0:T(8,128)} custom-call(f32[256,128]{1,0:T(8,128)} %mul.76.refs_0_, f32[256,128]{1,0:T(8,128)} %mul.79.refs_1_, f32[256,128]{1,0:T(8,128)} %mul.82.refs_2_, f32[16,32,512]{2,1,0:T(8,128)} %copy-done.1, f32[16,32,512]{2,1,0:T(8,128)} %copy-done.2, f32[16,32,512]{2,1,0:T(8,128)} %copy-done.3), custom_call_target="tpu_custom_call" | custom-call | flops 2415919104 | bytes 5242880 | tf_op jit(solution)/shard_map/apply/pallas_call | solution.py:143
  125.5 1.0 copy-done
  126.5 5.1 %apply.3 = f32[32,32,512]{2,1,0:T(8,128)} custom-call(f32[256,128]{1,0:T(8,128)} %mul.73.refs_0_, f32[16,32,512]{2,1,0:T(8,128)} %copy-done, f32[32,32,512]{2,1,0:T(8,128)} %apply.2.refs_2_), custom_call_target="tpu_custom_call" | custom-call | flops 805306368 | bytes 3145728 | tf_op jit(solution)/shard_map/apply/pallas_call | solution.py:143
  (39 shorter events, 4.7 us)
Async XLA Ops:
  4.9 31.0 %all-to-all-start.1 = ((f32[16,32,512]{2,1,0:T(8,128)}), f32[16,32,512]{2,1,0:T(8,128)S(1)}, u32[]{:S(2)}, u32[]{:S(2)}) async-start(f32[16,32,512]{2,1,0:T(8,128)} %smooth.5), calls=%async_computation.1 | async-start | bytes 2097152 | tf_op jit(solution)/shard_map/all_to_all | solution.py:168
  16.3 24.7 %copy-start.4 = (s32[2,64]{1,0:T(2,128)S(1)}, s32[2,64]{1,0:T(2,128)}, u32[]{:S(2)}) copy-start(s32[2,64]{1,0:T(2,128)} %param.4) | copy-start | bytes 1540
  36.0 10.4 %copy-start.1 = (f32[16,32,512]{2,1,0:T(8,128)}, f32[16,32,512]{2,1,0:T(8,128)S(1)}, u32[]{:S(2)}) copy-start(f32[16,32,512]{2,1,0:T(8,128)S(1)} %all-to-all-done.1.refs_3_) | copy-start | bytes 3145732
  36.0 29.7 %all-to-all-start.2 = ((f32[16,32,512]{2,1,0:T(8,128)}), f32[16,32,512]{2,1,0:T(8,128)S(1)}, u32[]{:S(2)}, u32[]{:S(2)}) async-start(f32[16,32,512]{2,1,0:T(8,128)} %smooth.6), calls=%async_computation.2 | async-start | bytes 2097152 | tf_op jit(solution)/shard_map/all_to_all | solution.py:168
  46.4 31.0 %copy-start.5 = (s32[32]{0:T(128)S(1)}, s32[32]{0:T(128)}, u32[]{:S(2)}) copy-start(s32[32]{0:T(128)} %param.5) | copy-start | bytes 388
  65.6 19.9 %copy-start.2 = (f32[16,32,512]{2,1,0:T(8,128)}, f32[16,32,512]{2,1,0:T(8,128)S(1)}, u32[]{:S(2)}) copy-start(f32[16,32,512]{2,1,0:T(8,128)S(1)} %all-to-all-done.2.refs_4_) | copy-start | bytes 3145732
  65.6 29.7 %all-to-all-start.3 = ((f32[16,32,512]{2,1,0:T(8,128)}), f32[16,32,512]{2,1,0:T(8,128)S(1)}, u32[]{:S(2)}, u32[]{:S(2)}) async-start(f32[16,32,512]{2,1,0:T(8,128)} %smooth.7), calls=%async_computation.3 | async-start | bytes 2097152 | tf_op jit(solution)/shard_map/all_to_all | solution.py:168
  95.3 7.8 %copy-start.3 = (f32[16,32,512]{2,1,0:T(8,128)}, f32[16,32,512]{2,1,0:T(8,128)S(1)}, u32[]{:S(2)}) copy-start(f32[16,32,512]{2,1,0:T(8,128)S(1)} %all-to-all-done.3.refs_5_) | copy-start | bytes 3145732
  95.3 30.2 %all-to-all-start = ((f32[16,32,512]{2,1,0:T(8,128)}), f32[16,32,512]{2,1,0:T(8,128)S(1)}, u32[]{:S(2)}, u32[]{:S(2)}) async-start(f32[16,32,512]{2,1,0:T(8,128)} %smooth.4), calls=%async_computation | async-start | bytes 2097152 | tf_op jit(solution)/shard_map/all_to_all | solution.py:168
  125.5 1.0 copy-start
